TPU v7x, 32 devices: a whole 2x2x4 slice. The times are simulated.
32 devices in a mesh: row: 4 (over z), col: 4 (over y, x), feat: 2 (over core).
Axes of the slice: x: 2, y: 2, z: 4, core: 2. Of those that a mesh axis runs over, the one named last changes fastest.
Arguments:
- tile_values: bfloat16 [4, 4, 80, 128, 128], P('row', 'col')
- tile_rows: int32 [4, 4, 80], P('row', 'col'), may hold values from 0 to 15, as said below
- tile_cols: int32 [4, 4, 80], P('row', 'col'), may hold values from 0 to 15
- tile_mask: int32 [4, 4, 80], P('row', 'col'), may hold values from 0 to 1, as said below
- degree_caps: int32 [8192], P(('row', 'col')), may hold values from 1 to 32, as said below
- clip_groups: int32 [8192], P(('row', 'col')), may hold values from 0 to 7
- clip_bounds: float32 [8], replicated, may hold values from 51.2 to 256
- features: bfloat16 [8192, 256], P('col', 'feat')
- weight: bfloat16 [256, 256], replicated, may hold values from -0.375 to 0.375
- out_grad: bfloat16 [8192, 256], P(('row', 'col'), 'feat')
- dp_noise: float32 [256, 256], P(None, 'feat'), may hold values from -6 to 6
Outputs:
- out_feat: bfloat16 [8192, 256], P(('row', 'col'), 'feat')
- grad_weight: float32 [256, 256], P(None, 'feat')
- grad_input: bfloat16 [8192, 256], P('col', 'feat')
Inputs may be any that keep to these rules, and one draw needn't show every extreme that they name: `tile_rows`: each tile slot of one pair of row and col indices names a distinct pair of block row and block column. `tile_mask`: at most all 80 slots of one pair of row and col indices are live; in every draw some pair has all of them live. degree_caps[i] is the number of nonzero entries in row i of A, raised to 1 where it is 0 and capped at 32.
All inputs are finite; a program needn't handle non-finite values.
Results may differ from a plain program's by a relative error of at most 0.006.
Values may be sent and summed in bfloat16 or wider, within the bound.
A program may use at most 128 MiB of HBM per device.

v0:
```python
import math
import jax
import jax.numpy as jnp
from jax import lax
from jax.sharding import PartitionSpec as P


def slot_products(tile_vals, take_ids, source, flipped):
    contraction = "kji,kjf->kif" if flipped else "kij,kjf->kif"
    slot_total = tile_vals.shape[0]
    picked = jnp.take(source, take_ids, axis=0)
    products = jnp.einsum(contraction, tile_vals, picked, preferred_element_type=jnp.float32)
    return (products, jnp.arange(slot_total, dtype=jnp.int32))


def block_sums(products, put_ids, live_slots, block_count):
    wanted = jnp.arange(block_count, dtype=jnp.int32)
    selector = ((put_ids[:, None] == wanted[None, :]) & live_slots[:, None]).astype(jnp.float32)
    return jnp.einsum("kb,kif->bif", selector, products, precision=lax.Precision.HIGHEST)


def per_device(
    tile_values,
    tile_rows,
    tile_cols,
    tile_mask,
    degree_caps,
    clip_groups,
    clip_bounds,
    features,
    weight,
    out_grad,
    dp_noise,
):
    tile_vals = tile_values[0, 0]
    row_ids = tile_rows[0, 0]
    col_ids = tile_cols[0, 0]
    tile_live = tile_mask[0, 0]
    block_size = tile_vals.shape[1]
    half_width = features.shape[1]
    node_count = out_grad.shape[0]
    col_devices = lax.axis_size("col")
    row_devices = lax.axis_size("row")
    row_blocks = node_count * col_devices // block_size
    col_blocks = features.shape[0] // block_size
    grad_scale = 1.0 / math.sqrt(node_count * col_devices * row_devices)
    source = features.reshape(col_blocks, block_size, half_width)
    products, order = slot_products(tile_vals, col_ids, source, False)
    put_rows = jnp.take(row_ids, order)
    live_rows = jnp.take(tile_live, order) == 1
    partial_value = block_sums(products, put_rows, live_rows, row_blocks)
    partial_value = partial_value.reshape(row_blocks * block_size, half_width)
    summed = lax.psum_scatter(partial_value, "col", scatter_dimension=0, tiled=True)
    node_scale = lax.rsqrt(degree_caps.astype(jnp.float32))[:, None]
    agg_half = (summed * node_scale).astype(jnp.bfloat16)
    aggregate = lax.all_gather(agg_half, "feat", axis=1, tiled=True)
    feat_idx = lax.axis_index("feat")
    weight_cols = lax.dynamic_slice_in_dim(weight, feat_idx * half_width, half_width, 1)
    weight_rows = lax.dynamic_slice_in_dim(weight, feat_idx * half_width, half_width, 0)
    pre_act = jnp.dot(aggregate, weight_cols, preferred_element_type=jnp.float32)
    out_feat = jax.nn.silu(pre_act).astype(jnp.bfloat16)
    gate_sig = jax.nn.sigmoid(pre_act)
    grad_pre = (
        out_grad.astype(jnp.float32) * gate_sig * (1.0 + pre_act * (1.0 - gate_sig))
    ).astype(jnp.bfloat16)
    grad_full = lax.all_gather(grad_pre, "feat", axis=1, tiled=True)
    agg_sq = jnp.sum(jnp.square(aggregate.astype(jnp.float32)), axis=1)
    grad_sq = jnp.sum(jnp.square(grad_full.astype(jnp.float32)), axis=1)
    group_hits = (
        clip_groups[:, None] == jnp.arange(clip_bounds.shape[0], dtype=jnp.int32)[None, :]
    ).astype(jnp.float32)
    bounds = jnp.sum(group_hits * clip_bounds[None, :], axis=1)
    factor = jnp.minimum(1.0, bounds / (jnp.sqrt(agg_sq + 1e-06) * jnp.sqrt(grad_sq + 1e-06)))
    clipped = (factor[:, None] * grad_pre.astype(jnp.float32)).astype(jnp.bfloat16)
    local_grad = lax.dot_general(
        aggregate, clipped, (((0,), (0,)), ((), ())), preferred_element_type=jnp.float32
    )
    grad_weight = lax.psum(local_grad, ("row", "col")) * grad_scale + dp_noise
    back_prod = lax.dot_general(
        grad_full, weight_rows, (((1,), (1,)), ((), ())), preferred_element_type=jnp.float32
    )
    grad_agg = (back_prod * node_scale).astype(jnp.bfloat16)
    range_grads = lax.all_gather(grad_agg, "col", axis=0, tiled=True)
    grad_source = range_grads.reshape(row_blocks, block_size, half_width)
    back_products, back_order = slot_products(tile_vals, row_ids, grad_source, True)
    put_cols = jnp.take(col_ids, back_order)
    live_cols = jnp.take(tile_live, back_order) == 1
    input_part = block_sums(back_products, put_cols, live_cols, col_blocks)
    input_part = input_part.reshape(col_blocks * block_size, half_width)
    grad_input = lax.psum(input_part, "row").astype(jnp.bfloat16)
    return (out_feat, grad_weight, grad_input)


def solution(mesh):
    placed = (
        P("row", "col", None, None, None),
        P("row", "col", None),
        P("row", "col", None),
        P("row", "col", None),
        P(("row", "col")),
        P(("row", "col")),
        P(),
        P("col", "feat"),
        P(),
        P(("row", "col"), "feat"),
        P(None, "feat"),
    )
    return jax.shard_map(
        per_device,
        mesh=mesh,
        in_specs=placed,
        out_specs=(P(("row", "col"), "feat"), P(None, "feat"), P("col", "feat")),
        check_vma=False,
    )
```

profile of v0, /device:TPU:0, one launch (start us, length us, event | category | flops | bytes accessed | tf_op | source)
XLA Modules:
  0.0 184.9 jit_solution(5821199909000592426)
XLA Ops:
  7.2 0.0 reduce-scatter.2.cloned.1.call-start
  7.2 0.9 compare_and_fusion.1
  8.1 0.7 compare_select_fusion.1
  8.8 1.6 gather_fusion.1
  10.4 1.6 gather_fusion
  12.0 2.5 %gather_fusion.2 = bf16[80,128,128]{2,1,0:T(8,128)(2,1)} fusion(bf16[16,128,128]{2,1,0:T(8,128)(2,1)S(1)} %bitcast.41, s32[1024]{0:T(1024)S(1)} %pad_clamp_fusion.1), kind=kCustom, calls=%fused_computation.1.clone | custom fusion | bytes 5243200 | tf_op jit(solution)/shard_map/jit(_take)/gather | solution.py:11
  14.6 6.2 %fusion.8 = f32[80,128,128]{1,2,0:T(8,128)} fusion(bf16[1,1,80,128,128]{4,3,2,1,0:T(8,128)(2,1)S(1)} %copy-done, bf16[80,128,128]{2,1,0:T(8,128)(2,1)} %gather_fusion.2, pred[80]{0:T(512)(128)(4,1)S(1)} %compare_and_fusion.1), kind=kOutput, calls=%fused_computation.13 | convolution fusion | flops 336855040 | bytes 10485840 | tf_op jit(solution)/shard_map/kij,kjf->kif/dot_general | solution.py:12
  20.7 6.4 %copy.21 = f32[80,128,128]{2,0,1:T(8,128)} copy(f32[80,128,128]{1,2,0:T(8,128)} %fusion.8) | data formatting | bytes 10485760 | tf_op jit(solution)/shard_map/kij,kjf->kif/dot_general | solution.py:12
  27.1 4.3 %fusion.28 = f32[16,128,128]{2,0,1:T(8,128)S(1)} fusion(f32[80,128,128]{2,0,1:T(8,128)} %copy.21, s32[80]{0:T(128)S(1)} %broadcast_select_fusion.1, pred[80]{0:T(512)(128)(4,1)S(1)} %select_compare_fusion), kind=kOutput, calls=%fused_computation.38 | convolution fusion | flops 251660800 | bytes 6291856 | tf_op jit(solution)/shard_map/kb,kif->bif/dot_general | solution.py:19
  31.5 1.3 copy.22
  32.8 0.0 reduce-scatter.2.cloned.1.call-update
  32.9 0.0 all-reduce.3.cloned.1.call-start
  32.9 1.2 gather_fusion.3
  34.2 0.1 select_reduce_fusion
  34.3 29.1 %reduce-scatter.2.cloned.1.call-done = f32[512,128]{1,0:T(8,128)} async-done(((f32[2048,128]{1,0:T(8,128)}), f32[512,128]{1,0:T(8,128)}) %reduce-scatter.2.cloned.1.call-update) | async-done | bytes 262160 | tf_op jit(solution)/shard_map/reduce_scatter | solution.py:53
  63.4 1.1 multiply_convert_fusion.3
  64.5 2.0 %all_gather.9 = bf16[512,256]{1,0:T(8,128)(2,1)S(1)} all-gather(bf16[512,128]{1,0:T(8,128)(2,1)S(1)} %multiply_convert_fusion.3), channel_id=1, replica_groups=mesh['row'=4,'col'=4,'feat'=2] {'feat'}, dimensions={1}, use_global_device_ids=true | all-gather | bytes 393216 | tf_op jit(solution)/shard_map/all_gather | solution.py:56
  66.5 0.1 multiply_reduce_fusion.1
  66.7 1.0 multiply_convert_fusion.1
  67.7 2.0 %all_gather.10 = bf16[512,256]{1,0:T(8,128)(2,1)S(1)} all-gather(bf16[512,128]{1,0:T(8,128)(2,1)S(1)} %get-tuple-element.5), channel_id=1, replica_groups=mesh['row'=4,'col'=4,'feat'=2] {'feat'}, dimensions={1}, use_global_device_ids=true | all-gather | bytes 393216 | tf_op jit(solution)/shard_map/all_gather | solution.py:66
  69.6 0.1 multiply_reduce_fusion
  69.8 0.2 fusion.20
  70.0 1.0 fusion.21
  71.1 10.2 %all_gather.11 = bf16[2048,128]{1,0:T(8,128)(2,1)S(1)} all-gather(bf16[512,128]{1,0:T(8,128)(2,1)S(1)} %fusion.20), channel_id=1, replica_groups=mesh['row'=4,'col'=4,'feat'=2] {'col'}, dimensions={0}, use_global_device_ids=true | all-gather | bytes 655360 | tf_op jit(solution)/shard_map/all_gather | solution.py:83
  81.3 2.5 %gather_fusion.4 = bf16[80,128,128]{2,1,0:T(8,128)(2,1)} fusion(bf16[16,128,128]{2,1,0:T(8,128)(2,1)S(1)} %bitcast.40, s32[1024]{0:T(1024)S(1)} %pad_clamp_fusion), kind=kCustom, calls=%fused_computation.4.clone | custom fusion | bytes 5243200 | tf_op jit(solution)/shard_map/jit(_take)/gather | solution.py:11
  83.8 5.2 %fusion.13 = f32[80,128,128]{1,2,0:T(8,128)} fusion(bf16[1,1,80,128,128]{4,3,2,1,0:T(8,128)(2,1)S(1)} %copy-done, bf16[80,128,128]{2,1,0:T(8,128)(2,1)} %gather_fusion.4, pred[80]{0:T(512)(128)(4,1)S(1)} %compare_and_fusion), kind=kOutput, calls=%fused_computation.14 | convolution fusion | flops 336855040 | bytes 10485840 | tf_op jit(solution)/shard_map/kji,kjf->kif/dot_general | solution.py:12
  89.0 6.4 %copy.24 = f32[80,128,128]{2,0,1:T(8,128)} copy(f32[80,128,128]{1,2,0:T(8,128)} %fusion.13) | data formatting | bytes 10485760 | tf_op jit(solution)/shard_map/kji,kjf->kif/dot_general | solution.py:12
  95.4 4.3 %fusion.32 = f32[16,128,128]{2,0,1:T(8,128)S(1)} fusion(f32[80,128,128]{2,0,1:T(8,128)} %copy.24, s32[80]{0:T(128)S(1)} %broadcast_select_fusion, pred[80]{0:T(512)(128)(4,1)S(1)} %select_compare_fusion), kind=kOutput, calls=%fused_computation.41 | convolution fusion | flops 251660800 | bytes 6291856 | tf_op jit(solution)/shard_map/kb,kif->bif/dot_general | solution.py:19
  99.8 1.3 copy.25
  101.1 44.6 %all-reduce.4 = bf16[2048,128]{1,0:T(8,128)(2,1)} all-reduce(f32[2048,128]{1,0:T(8,128)} %bitcast.43), channel_id=1, replica_groups=mesh['row'=4,'col'=4,'feat'=2] {'row'}, use_global_device_ids=true, to_apply=%region_5.8 | all-reduce | flops 262144 | bytes 1572864 | tf_op jit(solution)/shard_map/psum | solution.py:90
  145.7 30.7 %all-reduce.3.cloned.1.call-done = f32[256,128]{1,0:T(8,128)} async-done(((f32[256,128]{1,0:T(8,128)}), f32[256,128]{1,0:T(8,128)}) %all-reduce.3.cloned.1.call-update) | async-done | bytes 131088 | tf_op jit(solution)/shard_map/psum | solution.py:78
  176.5 1.6 multiply_add_fusion
  (32 shorter events, 0.1 us)
Async XLA Ops:
  7.2 7.4 %copy-start = (bf16[1,1,80,128,128]{4,3,2,1,0:T(8,128)(2,1)S(1)}, bf16[1,1,80,128,128]{4,3,2,1,0:T(8,128)(2,1)}, u32[]{:S(2)}) copy-start(bf16[1,1,80,128,128]{4,3,2,1,0:T(8,128)(2,1)} %param.15) | copy-start | bytes 7864324
  7.2 4.8 %copy-start.3 = (bf16[2048,128]{1,0:T(8,128)(2,1)S(1)}, bf16[2048,128]{1,0:T(8,128)(2,1)}, u32[]{:S(2)}) copy-start(bf16[2048,128]{1,0:T(8,128)(2,1)} %param.22) | copy-start | bytes 1572868
  7.2 56.3 %reduce-scatter.2.cloned.1.call-start = ((), (), s32[]{:S(2)}) async-start(), calls=%async_computation.1 | async-start | bytes 1310720 | tf_op jit(solution)/shard_map/reduce_scatter | solution.py:53
  31.5 1.5 copy-start.1
  31.5 2.7 %copy-start.2 = (s32[1,1,80]{2,1,0:T(1,128)S(1)}, s32[1,1,80]{2,1,0:T(1,128)}, u32[]{:S(2)}) copy-start(s32[1,1,80]{2,1,0:T(1,128)} %param.16) | copy-start | bytes 964
  31.5 2.7 %copy-start.6 = (s32[512]{0:T(512)S(1)}, s32[512]{0:T(512)}, u32[]{:S(2)}) copy-start(s32[512]{0:T(512)} %param.20) | copy-start | bytes 6148
  31.5 2.7 %copy-start.8 = (f32[8]{0:T(128)S(1)}, f32[8]{0:T(128)}, u32[]{:S(2)}) copy-start(f32[8]{0:T(128)} %param.21) | copy-start | bytes 100
  31.5 2.8 %copy-start.7 = (s32[512]{0:T(512)S(1)}, s32[512]{0:T(512)}, u32[]{:S(2)}) copy-start(s32[512]{0:T(512)} %param.19) | copy-start | bytes 6148
  31.5 35.2 %copy-start.5 = (bf16[256,256]{1,0:T(8,128)(2,1)S(1)}, bf16[256,256]{1,0:T(8,128)(2,1)}, u32[]{:S(2)}) copy-start(bf16[256,256]{1,0:T(8,128)(2,1)} %param.23) | copy-start | bytes 393220
  31.5 35.2 %copy-start.9 = (bf16[512,128]{1,0:T(8,128)(2,1)S(1)}, bf16[512,128]{1,0:T(8,128)(2,1)}, u32[]{:S(2)}) copy-start(bf16[512,128]{1,0:T(8,128)(2,1)} %param.24) | copy-start | bytes 393220
  32.9 143.6 %all-reduce.3.cloned.1.call-start = ((), (), s32[]{:S(2)}) async-start(), calls=%async_computation.2 | async-start | bytes 262144 | tf_op jit(solution)/shard_map/psum | solution.py:78
  99.8 76.7 %copy-start.4 = (f32[256,128]{1,0:T(8,128)S(1)}, f32[256,128]{1,0:T(8,128)}, u32[]{:S(2)}) copy-start(f32[256,128]{1,0:T(8,128)} %param.25) | copy-start | bytes 393220
Sparse Core Ops, SparseCore 0:
  33.0 30.4 reduce-scatter.1
  71.2 105.2 all-reduce.2
where the time goes:
time: 185 us
  waiting for transfers between devices  59.9 us (32%)
  blocking collectives  58.8 us (32%)
  local copies, waits for them, and re-layouts  24.9 us (13%)
  matrix products  22.3 us (12%)
  between operations  14.3 us (8%)
  other arithmetic  4.65 us (3%)
    psum x1, blocking collectives, per_device(): grad_input = lax.psum(input_part, 'row').astype(jnp.bfloat16)  44.6 us
    psum x1, waiting for transfers between devices, per_device(): grad_weight = lax.psum(local_grad, ('row', 'col')) * grad_scale + dp_noise  30.7 us
    reduce_scatter x1, waiting for transfers between devices, per_device(): lax.psum_scatter(partial_value, 'col', scatter_dimension=0, tiled=True)  29.1 us
    dot_general x2, local copies, waits for them, and re-layouts, slot_products(): jnp.einsum(contraction, tile_vals, picked, preferred_element_type=jnp.flo...  12.8 us
    dot_general x2, matrix products, slot_products(): jnp.einsum(contraction, tile_vals, picked, preferred_element_type=jnp.flo...  11.4 us
    all_gather x1, blocking collectives, per_device(): range_grads = lax.all_gather(grad_agg, 'col', axis=0, tiled=True)  10.2 us
    dot_general x2, matrix products, block_sums(): jnp.einsum('kb,kif->bif', selector, products, precision=lax.Precision.HIG...  8.69 us
    gather x2, local copies, waits for them, and re-layouts, slot_products(): picked = jnp.take(source, take_ids, axis=0)  5.08 us
  transfers between devices with their start and end apart: 2, of which 2 were waited for; matrix products, arithmetic and copies ran while one was open for 11% of the time, Pallas kernels for 0%

commit v1 on v0

--- a/solution.py
+++ b/solution.py
@@ -75,7 +75,7 @@
     local_grad = lax.dot_general(
         aggregate, clipped, (((0,), (0,)), ((), ())), preferred_element_type=jnp.float32
     )
-    grad_weight = lax.psum(local_grad, ("row", "col")) * grad_scale + dp_noise
+    grad_weight = lax.psum(lax.psum(local_grad, "col"), "row") * grad_scale + dp_noise
     back_prod = lax.dot_general(
         grad_full, weight_rows, (((1,), (1,)), ((), ())), preferred_element_type=jnp.float32
     )

time: 185 us -> 170 us (0.919)
  waiting for transfers between devices: 59.9 us -> 41 us
  blocking collectives: 58.8 us -> 63 us
    psum x1 -> x2, waiting for transfers between devices: 30.7 us -> 11.9 us  [the longest x1 11.9 us: per_device(): lax.psum(local_grad, 'col')]
    psum x1, blocking collectives: 44.6 us -> 48.5 us  [per_device(): grad_input = lax.psum(input_part, 'row').astype(jnp.bfloat16)]
  transfers between devices with their start and end apart: 2 -> 3, of which waited for: 2 -> 2; matrix products, arithmetic and copies ran while one was open for 11% -> 12% of each run, Pallas kernels for 0% -> 0%
where the time goes in v1:
time: 170 us
  blocking collectives  63 us (37%)
  waiting for transfers between devices  41 us (24%)
  local copies, waits for them, and re-layouts  24.9 us (15%)
  matrix products  22.3 us (13%)
  between operations  14 us (8%)
  other arithmetic  4.65 us (3%)
    psum x1, blocking collectives, per_device(): grad_input = lax.psum(input_part, 'row').astype(jnp.bfloat16)  48.5 us
    reduce_scatter x1, waiting for transfers between devices, per_device(): lax.psum_scatter(partial_value, 'col', scatter_dimension=0, tiled=True)  29.1 us
    dot_general x2, local copies, waits for them, and re-layouts, slot_products(): jnp.einsum(contraction, tile_vals, picked, preferred_element_type=jnp.flo...  12.8 us
    psum x1, waiting for transfers between devices, per_device(): lax.psum(local_grad, 'col')  11.9 us
    dot_general x2, matrix products, slot_products(): jnp.einsum(contraction, tile_vals, picked, preferred_element_type=jnp.flo...  11.3 us
    all_gather x1, blocking collectives, per_device(): range_grads = lax.all_gather(grad_agg, 'col', axis=0, tiled=True)  10.6 us
    dot_general x2, matrix products, block_sums(): jnp.einsum('kb,kif->bif', selector, products, precision=lax.Precision.HIG...  8.72 us
    gather x2, local copies, waits for them, and re-layouts, slot_products(): picked = jnp.take(source, take_ids, axis=0)  5.08 us
  transfers between devices with their start and end apart: 3, of which 2 were waited for; matrix products, arithmetic and copies ran while one was open for 12% of the time, Pallas kernels for 0%

profile of v1, /device:TPU:0, one launch (start us, length us, event | category | flops | bytes accessed | tf_op | source)
XLA Modules:
  0.0 170.0 jit_solution(17492524436314618150)
XLA Ops:
  7.2 0.0 reduce-scatter.2.cloned.1.call-start
  7.2 0.9 compare_and_fusion.1
  8.1 0.7 compare_select_fusion.1
  8.8 1.6 gather_fusion.1
  10.4 1.6 gather_fusion
  12.0 2.5 %gather_fusion.2 = bf16[80,128,128]{2,1,0:T(8,128)(2,1)} fusion(bf16[16,128,128]{2,1,0:T(8,128)(2,1)S(1)} %bitcast.41, s32[1024]{0:T(1024)S(1)} %pad_clamp_fusion.1), kind=kCustom, calls=%fused_computation.1.clone | custom fusion | bytes 5243200 | tf_op jit(solution)/shard_map/jit(_take)/gather | solution.py:11
  14.6 6.2 %fusion.8 = f32[80,128,128]{1,2,0:T(8,128)} fusion(bf16[1,1,80,128,128]{4,3,2,1,0:T(8,128)(2,1)S(1)} %copy-done, bf16[80,128,128]{2,1,0:T(8,128)(2,1)} %gather_fusion.2, pred[80]{0:T(512)(128)(4,1)S(1)} %compare_and_fusion.1), kind=kOutput, calls=%fused_computation.13 | convolution fusion | flops 336855040 | bytes 10485840 | tf_op jit(solution)/shard_map/kij,kjf->kif/dot_general | solution.py:12
  20.7 6.4 %copy.21 = f32[80,128,128]{2,0,1:T(8,128)} copy(f32[80,128,128]{1,2,0:T(8,128)} %fusion.8) | data formatting | bytes 10485760 | tf_op jit(solution)/shard_map/kij,kjf->kif/dot_general | solution.py:12
  27.1 4.3 %fusion.28 = f32[16,128,128]{2,0,1:T(8,128)S(1)} fusion(f32[80,128,128]{2,0,1:T(8,128)} %copy.21, s32[80]{0:T(128)S(1)} %broadcast_select_fusion.1, pred[80]{0:T(512)(128)(4,1)S(1)} %select_compare_fusion), kind=kOutput, calls=%fused_computation.38 | convolution fusion | flops 251660800 | bytes 6291856 | tf_op jit(solution)/shard_map/kb,kif->bif/dot_general | solution.py:19
  31.5 1.3 copy.22
  32.9 0.0 all-reduce.4.cloned.1.call-start
  32.9 1.2 gather_fusion.3
  34.2 0.1 select_reduce_fusion
  34.3 29.1 %reduce-scatter.2.cloned.1.call-done = f32[512,128]{1,0:T(8,128)} async-done(((f32[2048,128]{1,0:T(8,128)}), f32[512,128]{1,0:T(8,128)}) %reduce-scatter.2.cloned.1.call-update) | async-done | bytes 262160 | tf_op jit(solution)/shard_map/reduce_scatter | solution.py:53
  63.4 1.1 multiply_convert_fusion.3
  64.5 2.0 %all_gather.9 = bf16[512,256]{1,0:T(8,128)(2,1)S(1)} all-gather(bf16[512,128]{1,0:T(8,128)(2,1)S(1)} %multiply_convert_fusion.3), channel_id=1, replica_groups=mesh['row'=4,'col'=4,'feat'=2] {'feat'}, dimensions={1}, use_global_device_ids=true | all-gather | bytes 393216 | tf_op jit(solution)/shard_map/all_gather | solution.py:56
  66.5 0.1 multiply_reduce_fusion.1
  66.7 1.0 multiply_convert_fusion.1
  67.7 2.0 %all_gather.10 = bf16[512,256]{1,0:T(8,128)(2,1)S(1)} all-gather(bf16[512,128]{1,0:T(8,128)(2,1)S(1)} %get-tuple-element.5), channel_id=1, replica_groups=mesh['row'=4,'col'=4,'feat'=2] {'feat'}, dimensions={1}, use_global_device_ids=true | all-gather | bytes 393216 | tf_op jit(solution)/shard_map/all_gather | solution.py:66
  69.6 0.1 multiply_reduce_fusion
  69.8 0.2 fusion.20
  70.0 1.0 fusion.21
  71.1 0.0 all-reduce.6.cloned.1.call-start
  71.1 10.6 %all_gather.11 = bf16[2048,128]{1,0:T(8,128)(2,1)S(1)} all-gather(bf16[512,128]{1,0:T(8,128)(2,1)S(1)} %fusion.20), channel_id=1, replica_groups=mesh['row'=4,'col'=4,'feat'=2] {'col'}, dimensions={0}, use_global_device_ids=true | all-gather | bytes 655360 | tf_op jit(solution)/shard_map/all_gather | solution.py:83
  81.7 2.5 %gather_fusion.4 = bf16[80,128,128]{2,1,0:T(8,128)(2,1)} fusion(bf16[16,128,128]{2,1,0:T(8,128)(2,1)S(1)} %bitcast.40, s32[1024]{0:T(1024)S(1)} %pad_clamp_fusion), kind=kCustom, calls=%fused_computation.4.clone | custom fusion | bytes 5243200 | tf_op jit(solution)/shard_map/jit(_take)/gather | solution.py:11
  84.2 5.2 %fusion.13 = f32[80,128,128]{1,2,0:T(8,128)} fusion(bf16[1,1,80,128,128]{4,3,2,1,0:T(8,128)(2,1)S(1)} %copy-done, bf16[80,128,128]{2,1,0:T(8,128)(2,1)} %gather_fusion.4, pred[80]{0:T(512)(128)(4,1)S(1)} %compare_and_fusion), kind=kOutput, calls=%fused_computation.14 | convolution fusion | flops 336855040 | bytes 10485840 | tf_op jit(solution)/shard_map/kji,kjf->kif/dot_general | solution.py:12
  89.4 6.4 %copy.24 = f32[80,128,128]{2,0,1:T(8,128)} copy(f32[80,128,128]{1,2,0:T(8,128)} %fusion.13) | data formatting | bytes 10485760 | tf_op jit(solution)/shard_map/kji,kjf->kif/dot_general | solution.py:12
  95.8 4.4 %fusion.32 = f32[16,128,128]{2,0,1:T(8,128)S(1)} fusion(f32[80,128,128]{2,0,1:T(8,128)} %copy.24, s32[80]{0:T(128)S(1)} %broadcast_select_fusion, pred[80]{0:T(512)(128)(4,1)S(1)} %select_compare_fusion), kind=kOutput, calls=%fused_computation.41 | convolution fusion | flops 251660800 | bytes 6291856 | tf_op jit(solution)/shard_map/kb,kif->bif/dot_general | solution.py:19
  100.2 1.3 copy.25
  101.5 11.9 %all-reduce.4.cloned.1.call-done = f32[256,128]{1,0:T(8,128)} async-done(((f32[256,128]{1,0:T(8,128)}), f32[256,128]{1,0:T(8,128)}) %all-reduce.4.cloned.1.call-update) | async-done | bytes 131088 | tf_op jit(solution)/shard_map/psum | solution.py:78
  113.4 48.5 %all-reduce.7 = bf16[2048,128]{1,0:T(8,128)(2,1)} all-reduce(f32[2048,128]{1,0:T(8,128)} %bitcast.43), channel_id=1, replica_groups=mesh['row'=4,'col'=4,'feat'=2] {'row'}, use_global_device_ids=true, to_apply=%region_6.9 | all-reduce | flops 262144 | bytes 1572864 | tf_op jit(solution)/shard_map/psum | solution.py:90
  161.9 1.6 multiply_add_fusion
  (35 shorter events, 0.2 us)
Async XLA Ops:
  7.2 7.4 %copy-start = (bf16[1,1,80,128,128]{4,3,2,1,0:T(8,128)(2,1)S(1)}, bf16[1,1,80,128,128]{4,3,2,1,0:T(8,128)(2,1)}, u32[]{:S(2)}) copy-start(bf16[1,1,80,128,128]{4,3,2,1,0:T(8,128)(2,1)} %param.15) | copy-start | bytes 7864324
  7.2 4.8 %copy-start.3 = (bf16[2048,128]{1,0:T(8,128)(2,1)S(1)}, bf16[2048,128]{1,0:T(8,128)(2,1)}, u32[]{:S(2)}) copy-start(bf16[2048,128]{1,0:T(8,128)(2,1)} %param.22) | copy-start | bytes 1572868
  7.2 56.3 %reduce-scatter.2.cloned.1.call-start = ((), (), s32[]{:S(2)}) async-start(), calls=%async_computation.1 | async-start | bytes 1310720 | tf_op jit(solution)/shard_map/reduce_scatter | solution.py:53
  31.5 1.5 copy-start.1
  31.5 2.7 %copy-start.2 = (s32[1,1,80]{2,1,0:T(1,128)S(1)}, s32[1,1,80]{2,1,0:T(1,128)}, u32[]{:S(2)}) copy-start(s32[1,1,80]{2,1,0:T(1,128)} %param.16) | copy-start | bytes 964
  31.5 2.7 %copy-start.6 = (s32[512]{0:T(512)S(1)}, s32[512]{0:T(512)}, u32[]{:S(2)}) copy-start(s32[512]{0:T(512)} %param.20) | copy-start | bytes 6148
  31.5 2.7 %copy-start.8 = (f32[8]{0:T(128)S(1)}, f32[8]{0:T(128)}, u32[]{:S(2)}) copy-start(f32[8]{0:T(128)} %param.21) | copy-start | bytes 100
  31.5 2.8 %copy-start.7 = (s32[512]{0:T(512)S(1)}, s32[512]{0:T(512)}, u32[]{:S(2)}) copy-start(s32[512]{0:T(512)} %param.19) | copy-start | bytes 6148
  31.5 35.2 %copy-start.5 = (bf16[256,256]{1,0:T(8,128)(2,1)S(1)}, bf16[256,256]{1,0:T(8,128)(2,1)}, u32[]{:S(2)}) copy-start(bf16[256,256]{1,0:T(8,128)(2,1)} %param.23) | copy-start | bytes 393220
  31.5 35.2 %copy-start.9 = (bf16[512,128]{1,0:T(8,128)(2,1)S(1)}, bf16[512,128]{1,0:T(8,128)(2,1)}, u32[]{:S(2)}) copy-start(bf16[512,128]{1,0:T(8,128)(2,1)} %param.24) | copy-start | bytes 393220
  32.9 80.5 %all-reduce.4.cloned.1.call-start = ((), (), s32[]{:S(2)}) async-start(), calls=%async_computation.2 | async-start | bytes 262144 | tf_op jit(solution)/shard_map/psum | solution.py:78
  71.1 90.8 %all-reduce.6.cloned.1.call-start = ((), (), s32[]{:S(2)}) async-start(), calls=%async_computation.3 | async-start | bytes 262144 | tf_op jit(solution)/shard_map/psum | solution.py:78
  100.2 61.7 %copy-start.4 = (f32[256,128]{1,0:T(8,128)S(1)}, f32[256,128]{1,0:T(8,128)}, u32[]{:S(2)}) copy-start(f32[256,128]{1,0:T(8,128)} %param.25) | copy-start | bytes 393220
Sparse Core Ops, SparseCore 0:
  33.0 30.4 reduce-scatter.1
  71.2 42.1 all-reduce.3
  115.7 36.5 all-reduce.5
